TPU v7x, 32 devices: a whole 2x2x4 slice. The times are simulated.
32 devices in a mesh: sp: 8 (over y, x, core), ch: 4 (over z).
Axes of the slice: x: 2, y: 2, z: 4, core: 2. Of those that a mesh axis runs over, the one named last changes fastest.
Arguments:
- features: bfloat16 [64, 64, 2, 2, 14, 128], P(None, ('sp', 'ch')), may hold values from -6 to 6
- pre_act: bfloat16 [128, 32, 14, 128], P(None, ('sp', 'ch')), may hold values from -6 to 6
- cotangent: bfloat16 [128, 32, 14, 128], P(None, ('sp', 'ch')), may hold values from -12 to 12
- weight: bfloat16 [27, 64, 128], replicated, may hold values from -0.15625 to 0.15625
Outputs:
- data_grad: bfloat16 [64, 64, 2, 2, 14, 128], P(None, ('sp', 'ch'))
- weight_grad: float32 [27, 64, 128], replicated
All inputs are finite; a program needn't handle non-finite values.
Results may differ from a plain program's by a relative error of at most 0.0025.
Values may be sent and summed in bfloat16 or wider, within the bound.
A program may use at most 64 MiB of HBM per device.

v0:
```python
import math

import jax
import jax.numpy as jnp
from jax import lax
from jax.sharding import PartitionSpec as P


def shifted_2(block, axis, distance):
    devices = range(lax.axis_size(axis))
    route = [(i - distance, i) for i in devices if i - distance in devices]
    return lax.ppermute(block, axis, route)


def shifted(grad_plane, down, right):
    if down:
        grad_plane = jnp.concatenate([grad_plane[:, 1:], jnp.zeros_like(grad_plane[:, :1])], 1)
    if right:
        grad_plane = jnp.concatenate([grad_plane[..., 1:], jnp.zeros_like(grad_plane[..., :1])], -1)
    return grad_plane


def shift_set(grad_plane):
    result = {}
    for down in (0, 1):
        for right in (0, 1):
            result[down, right] = shifted(grad_plane, down, right).reshape(grad_plane.shape[0], -1)
    return result


def tap_parts(tap_pos):
    return (0 if tap_pos == 1 else 1, 1 if tap_pos == 0 else 0)


def weight_terms(depth_planes, grad_set, depth_taps):
    tap_terms = []
    for depth_tap in depth_taps:
        plane = depth_planes[depth_tap]
        for row_tap in range(3):
            row_par, down = tap_parts(row_tap)
            for col_tap in range(3):
                col_par, right = tap_parts(col_tap)
                tap_rows = plane[:, row_par, col_par].reshape(plane.shape[0], -1)
                tap_terms.append(
                    lax.dot_general(
                        tap_rows,
                        grad_set[down, right],
                        (((1,), (1,)), ((), ())),
                        preferred_element_type=jnp.float32,
                    )
                )
    return jnp.stack(tap_terms)


def data_terms(weight, here_set, next_set, out_rows, out_cols):
    chans = weight.shape[1]
    groups = {}
    for depth_tap in range(3):
        depth_par = 0 if depth_tap == 1 else 1
        source = next_set if depth_tap == 0 else here_set
        for row_tap in range(3):
            row_par, down = tap_parts(row_tap)
            for col_tap in range(3):
                col_par, right = tap_parts(col_tap)
                key = (depth_par, row_par, col_par)
                if key not in groups:
                    groups[key] = ([], [])
                groups[key][0].append(weight[depth_tap * 9 + row_tap * 3 + col_tap])
                groups[key][1].append(source[down, right])
    results = {}
    for key, pair in groups.items():
        w_rows = jnp.concatenate(pair[0], 1)
        results[key] = jnp.dot(
            w_rows, jnp.concatenate(pair[1], 0), preferred_element_type=jnp.float32
        ).reshape(chans, out_rows, out_cols)
    depth_parts = []
    for depth_par in range(2):
        row_parts = []
        for row_par in range(2):
            row_parts.append(
                jnp.stack([results[depth_par, row_par, 0], results[depth_par, row_par, 1]], 1)
            )
        depth_parts.append(jnp.stack(row_parts, 1))
    return jnp.stack(depth_parts, 1).astype(jnp.bfloat16)


def on_device(features, pre_act, cotangent, weight):
    masked = jnp.where(pre_act > 0, cotangent, jnp.zeros_like(cotangent))
    planes, out_rows, out_cols = (masked.shape[1], masked.shape[2], masked.shape[3])
    here = masked[:, 0]
    above_plane = shifted_2(here, ("sp", "ch"), -1)
    here_set = shift_set(here)
    next_set = shift_set(above_plane)
    below_plane = shifted_2(features[:, 1], ("sp", "ch"), 1)
    depth_planes = {0: below_plane, 1: features[:, 0], 2: features[:, 1]}
    grad_part = weight_terms(depth_planes, here_set, (0, 1, 2))
    data_grad = data_terms(weight, here_set, next_set, out_rows, out_cols)
    loss_scale = 1.0 / math.sqrt(
        lax.axis_size("sp") * lax.axis_size("ch") * planes * out_rows * out_cols
    )
    grouped = lax.psum_scatter(grad_part, "ch", scatter_dimension=1, tiled=True)
    share = lax.psum(grouped, "sp")
    summed = lax.all_gather(share, "ch", axis=1, tiled=True)
    return (data_grad, summed * loss_scale)


def solution(mesh):
    return jax.shard_map(
        on_device,
        mesh=mesh,
        in_specs=(
            P(None, ("sp", "ch"), None, None, None, None),
            P(None, ("sp", "ch"), None, None),
            P(None, ("sp", "ch"), None, None),
            P(),
        ),
        out_specs=(P(None, ("sp", "ch"), None, None, None, None), P()),
        check_vma=False,
    )
```

profile of v0, /device:TPU:0, one launch (start us, length us, event | category | flops | bytes accessed | tf_op | source)
XLA Modules:
  0.0 183.1 jit_solution(2299996503300104439)
XLA Ops:
  7.2 1.3 copy.15
  8.5 1.3 copy.14
  9.9 1.3 collective-permute-start
  11.2 3.7 %slice_bitcast_fusion = (bf16[64,2,2,14,128]{4,2,3,1,0:T(2,128)(2,1)}, bf16[64,2,2,14,128]{4,2,3,1,0:T(2,128)(2,1)S(1)}) fusion(bf16[64,2,2,2,14,128]{5,3,4,2,1,0:T(2,128)(2,1)} %param.4), kind=kLoop, calls=%fused_computation.83 | loop fusion | bytes 3670016 | tf_op jit(solution)/shard_map/squeeze | solution.py:95
  14.9 6.5 %collective-permute-start.1 = (bf16[64,2,2,14,128]{4,2,3,1,0:T(2,128)(2,1)S(1)}, bf16[64,2,2,14,128]{4,2,3,1,0:T(2,128)(2,1)}, u32[]{:S(2)}, u32[]{:S(2)}) collective-permute-start(bf16[64,2,2,14,128]{4,2,3,1,0:T(2,128)(2,1)S(1)} %get-tuple-element.17), channel_id=1, source_target_pairs={{0,1},{1,2},{2,3},{3,4},{4,5},{5,6},{6,7},{7,8},{8,9},{9,10},{10,1... | collective-permute-start | bytes 2752520 | tf_op jit(solution)/shard_map/ppermute | solution.py:12
  28.2 1.7 fusion
  29.9 1.1 convolution_convert_fusion.6
  31.0 1.1 stack_reshape.33
  32.2 1.8 %stack_reshape.32 = bf16[64,1,14,128]{3,2,0,1:T(8,128)(2,1)} reshape(bf16[64,1792]{1,0:T(8,128)(2,1)} %fusion) | data formatting | bytes 458752 | tf_op jit(solution)/shard_map/stack;reshape | solution.py:81
  34.0 2.1 %convolution_convert_fusion.4 = bf16[64,1792]{1,0:T(8,128)(2,1)} fusion(bf16[128,1792]{0,1:T(8,128)(2,1)S(1)} %bitcast.357, bf16[128,1792]{0,1:T(8,128)(2,1)S(1)} %bitcast.386, bf16[128,1792]{0,1:T(8,128)(2,1)S(1)} %bitcast.375, bf16[128,1792]{0,1:T(8,128)(2,1)S(1)} %bitcast.395, bf16[64,128]{1,0:T(8,128)(2,1)} %get-tuple-element.29, ...), kind=kOutput, calls=%fused_computation.7 | convolution fusion | flops 125157376 | bytes 2129920 | tf_op jit(solution)/shard_map/dot_general | solution.py:73
  36.1 1.8 %stack_reshape.35 = bf16[64,1,14,128]{3,2,0,1:T(8,128)(2,1)} reshape(bf16[64,1792]{1,0:T(8,128)(2,1)} %convolution_convert_fusion.4) | data formatting | bytes 458752 | tf_op jit(solution)/shard_map/stack;reshape | solution.py:81
  38.0 1.8 %convolution_convert_fusion.5 = bf16[64,1792]{1,0:T(8,128)(2,1)} fusion(bf16[128,1792]{0,1:T(8,128)(2,1)S(1)} %bitcast.358, bf16[128,1792]{0,1:T(8,128)(2,1)S(1)} %bitcast.376, bf16[64,128]{1,0:T(8,128)(2,1)} %get-tuple-element.33, bf16[64,128]{1,0:T(8,128)(2,1)} %get-tuple-element.34), kind=kOutput, calls=%fused_computation.8 | convolution fusion | flops 60735488 | bytes 1179648 | tf_op jit(solution)/shard_map/dot_general | solution.py:73
  39.8 1.8 stack_reshape.34
  41.6 1.4 maximum_bitcast_fusion.2
  43.0 1.2 maximum_bitcast_fusion
  44.2 10.8 %slice_reduce_fusion = (bf16[64,14,128]{2,1,0:T(8,128)(2,1)S(1)}, bf16[64,14,128]{2,1,0:T(8,128)(2,1)S(1)}, bf16[64,14,128]{2,1,0:T(8,128)(2,1)S(1)}, bf16[64,14...) fusion(bf16[64,2,2,14,128]{4,2,3,1,0:T(2,128)(2,1)S(1)} %get-tu, ...), kind=kLoop, calls=%fused_computation.90 | loop fusion | bytes 3670016 | tf_op jit(solution)/shard_map/slice | solution.py:43
  57.1 1.8 copy-done.1
  58.9 6.6 %slice_reduce_fusion.8 = (bf16[64,14,128]{2,1,0:T(8,128)(2,1)S(1)}, bf16[64,14,128]{2,1,0:T(8,128)(2,1)S(1)}, bf16[64,14,128]{2,1,0:T(8,128)(2,1)S(1)}, bf16[64,14,128]{2,1,0:T(8,128)(2,1)S(1)}) fusion(bf16[64,2,2,14,128]{4,2,3,1,0:T(2,128)(2,1)} %collective-permute-done.1), kind=kLoop, calls=%fused_computation.98 | loop fusion | bytes 1835008 | tf_op jit(solution)/shard_map/slice | solution.py:43
  76.8 3.3 %convolution_convert_fusion = bf16[64,1792]{1,0:T(8,128)(2,1)S(1)} fusion(bf16[64,1024]{1,0:T(8,128)(2,1)} %copy-done.7, bf16[1024,1792]{0,1:T(8,128)(2,1)} %constant_dynamic-update-slice_fusion.8), kind=kOutput, calls=%fused_computation.3 | convolution fusion | flops 234995712 | bytes 4030464 | tf_op jit(solution)/shard_map/dot_general | solution.py:73
  81.6 18.1 %reduce-scatter.2.cloned.1.call-done = f32[27,16,128]{2,1,0:T(8,128)} async-done(((f32[27,64,128]{2,1,0:T(8,128)}), f32[27,16,128]{2,1,0:T(8,128)}) %reduce-scatter.2.cloned.1.call-update) | async-done | bytes 221200 | tf_op jit(solution)/shard_map/reduce_scatter | solution.py:101
  100.1 4.1 %copy.16 = bf16[64,2,2,2,14,128]{5,3,4,2,1,0:T(2,128)(2,1)} copy(bf16[64,2,2,2,14,128]{5,4,0,3,2,1:T(8,128)(2,1)S(1)} %pad_maximum_fusion.7) | data formatting | bytes 3670016
  104.2 50.1 %all-reduce.8.cloned.1.call-done = f32[27,16,128]{2,1,0:T(8,128)} async-done(((f32[27,16,128]{2,1,0:T(8,128)}), f32[27,16,128]{2,1,0:T(8,128)}) %all-reduce.8.cloned.1.call-update) | async-done | bytes 221200 | tf_op jit(solution)/shard_map/psum | solution.py:102
  154.3 20.9 %all_gather.3 = f32[27,64,128]{2,1,0:T(8,128)S(1)} all-gather(f32[27,16,128]{2,1,0:T(8,128)} %all-reduce.8.cloned.1.call-done), channel_id=1, replica_groups=mesh['sp'=8,'ch'=4] {'ch'}, dimensions={1}, use_global_device_ids=true | all-gather | bytes 1105920 | tf_op jit(solution)/shard_map/all_gather | solution.py:103
  175.2 1.0 broadcast_multiply_fusion
  (98 shorter events, 21.8 us)
Async XLA Ops:
  7.2 92.5 %reduce-scatter.2.cloned.1.call-start = ((), (), s32[]{:S(2)}) async-start(), calls=%async_computation.1 | async-start | bytes 1105920 | tf_op jit(solution)/shard_map/reduce_scatter | solution.py:101
  8.5 13.0 %copy-start.6 = (bf16[27,64,128]{2,1,0:T(8,128)(2,1)S(1)}, bf16[27,64,128]{2,1,0:T(8,128)(2,1)}, u32[]{:S(2)}) copy-start(bf16[27,64,128]{2,1,0:T(8,128)(2,1)} %param.7) | copy-start | bytes 1327108
  9.9 45.1 %collective-permute-start = (bf16[128,14,128]{0,2,1:T(8,128)(2,1)S(1)}, bf16[128,14,128]{0,2,1:T(8,128)(2,1)S(1)}, u32[]{:S(2)}, u32[]{:S(2)}) collective-permute-start(bf16[128,14,128]{0,2,1:T(8,128)(2,1)S(1)} %bitcast.352), channel_id=1, source_target_pairs={{1,0},{2,1},{3,2},{4,3},{5,4},{6,5},{7,6},{8,7},{9,8},{10,9},{11,1... | collective-permute-start | bytes 1376264 | tf_op jit(solution)/shard_map/ppermute | solution.py:12
  14.9 44.0 %collective-permute-start.1 = (bf16[64,2,2,14,128]{4,2,3,1,0:T(2,128)(2,1)S(1)}, bf16[64,2,2,14,128]{4,2,3,1,0:T(2,128)(2,1)}, u32[]{:S(2)}, u32[]{:S(2)}) collective-permute-start(bf16[64,2,2,14,128]{4,2,3,1,0:T(2,128)(2,1)S(1)} %get-tuple-element.17), channel_id=1, source_target_pairs={{0,1},{1,2},{2,3},{3,4},{4,5},{5,6},{6,7},{7,8},{8,9},{9,10},{10,1... | collective-permute-start | bytes 2752520 | tf_op jit(solution)/shard_map/ppermute | solution.py:12
  27.6 0.7 copy-start.7
  41.6 2.6 %copy-start = (bf16[64,2,2,14,128]{4,2,3,1,0:T(2,128)(2,1)S(1)}, bf16[64,2,2,14,128]{4,2,3,1,0:T(2,128)(2,1)}, u32[]{:S(2)}) copy-start(bf16[64,2,2,14,128]{4,2,3,1,0:T(2,128)(2,1)} %get-tuple-element.16) | copy-start | bytes 2752516
  55.0 0.7 copy-start.9
  55.0 0.7 copy-start.10
  55.0 0.7 copy-start.11
  55.0 0.7 copy-start.12
  55.3 1.3 copy-start.3
  57.1 1.8 copy-start.1
  69.3 3.2 %copy-start.8 = (bf16[64,128]{1,0:T(8,128)(2,1)S(1)}, bf16[64,128]{1,0:T(8,128)(2,1)}, u32[]{:S(2)}) copy-start(bf16[64,128]{1,0:T(8,128)(2,1)} %get-tuple-element.28) | copy-start | bytes 49156
  71.3 0.9 copy-start.5
  72.2 82.1 %all-reduce.8.cloned.1.call-start = ((), (), s32[]{:S(2)}) async-start(), calls=%async_computation.2 | async-start | bytes 442368 | tf_op jit(solution)/shard_map/psum | solution.py:102
  74.2 6.1 %copy-start.4 = (bf16[128,14,128]{0,2,1:T(8,128)(2,1)S(1)}, bf16[128,14,128]{0,2,1:T(8,128)(2,1)}, u32[]{:S(2)}) copy-start(bf16[128,14,128]{0,2,1:T(8,128)(2,1)} %copy-done.3) | copy-start | bytes 1376260
  81.0 18.7 %copy-start.2 = (bf16[64,1,2,2,14,128]{5,4,0,3,2,1:T(8,128)(2,1)S(1)}, bf16[64,1,2,2,14,128]{5,4,0,3,2,1:T(8,128)(2,1)}, u32[]{:S(2)}) copy-start(bf16[64,1,2,2,14,128]{5,4,0,3,2,1:T(8,128)(2,1)} %maximum_bitcast_fusion) | copy-start | bytes 2752516
Sparse Core Ops, SparseCore 0:
  72.4 27.2 reduce-scatter.1
  102.8 51.4 all-reduce.7
where the time goes:
time: 185 us; the launch traced here: 183 us
  waiting for transfers between devices  68.2 us (37%)
  local copies, waits for them, and re-layouts  49.3 us (27%)
  blocking collectives  20.9 us (11%)
  matrix products  17.5 us (9%)
  between operations  14.6 us (8%)
  starting transfers between devices  8.1 us (4%)
  other arithmetic  4.44 us (2%)
    psum x1, waiting for transfers between devices, on_device(): share = lax.psum(grouped, 'sp')  50.1 us
    all_gather x1, blocking collectives, on_device(): summed = lax.all_gather(share, 'ch', axis=1, tiled=True)  20.9 us
    reduce_scatter x1, waiting for transfers between devices, on_device(): grouped = lax.psum_scatter(grad_part, 'ch', scatter_dimension=1, tiled=True)  18.1 us
    unnamed x43, local copies, waits for them, and re-layouts  17.8 us
    slice x2, local copies, waits for them, and re-layouts, weight_terms(): tap_rows = plane[:, row_par, col_par].reshape(plane.shape[0], -1)  17.4 us
    dot_general x8, matrix products, data_terms(): jnp.dot(w_rows, jnp.concatenate(pair[1], 0), preferred_element_type=jnp.f...  11.9 us
    ppermute x2, starting transfers between devices, shifted_2(): return lax.ppermute(block, axis, route)  7.8 us
    another operation x8, local copies, waits for them, and re-layouts, data_terms(): jnp.stack([results[depth_par, row_par, 0], results[depth_par, row_par, 1]...  7.39 us
  transfers between devices with their start and end apart: 4, of which 2 were waited for; matrix products, arithmetic and copies ran while one was open for 28% of the time, Pallas kernels for 0%

commit v1 on v0

v1 whole, which is shorter than its diff:
```python
import functools
import math

import jax
import jax.numpy as jnp
from jax import lax
from jax.experimental import pallas as pl
from jax.experimental.pallas import tpu as pltpu
from jax.sharding import PartitionSpec as P

MESH = pl.DeviceIdType.MESH
LANES = 128
UNIT = 8


def kernel(cfg, pre_hbm, cot_hbm, feat_hbm, w_hbm, dg_hbm, wg_hbm, *scr):
    (pre_v, cot_v, feat_v, w_v, m_nat, h_nat, f32s, m32, mh, mn, feat_a, dg_v, grad, out_v) = scr[:14]
    r1, r2, r3 = scr[14:17]
    in_sem, out_sem, halo_s, halo_r, sA, rA = scr[17:]
    chips, chs, rows, c_in, c_out, scale, chunks, taps_first = cfg
    sp = lax.axis_index("sp")
    ch = lax.axis_index("ch")
    chip = sp // 2
    core = sp % 2
    flat = sp * chs + ch
    last = chips * 2 * chs - 1
    span = rows * LANES

    loads = [
        pltpu.make_async_copy(pre_hbm, pre_v, in_sem.at[0]),
        pltpu.make_async_copy(cot_hbm, cot_v, in_sem.at[1]),
        pltpu.make_async_copy(feat_hbm, feat_v, in_sem.at[2]),
        pltpu.make_async_copy(w_hbm, w_v, in_sem.at[3]),
    ]
    for ld in loads:
        ld.start()

    bar = pltpu.get_barrier_semaphore()
    pl.semaphore_signal(bar, inc=1, device_id=(sp + 1 - 2 * core, ch), device_id_type=MESH)
    for k in range(1, chips):
        pl.semaphore_signal(bar, inc=1, device_id=(((chip + k) % chips) * 2 + core, ch), device_id_type=MESH)
    for k in range(1, chs):
        pl.semaphore_signal(bar, inc=1, device_id=(sp, (ch + k) % chs), device_id_type=MESH)
    prev = jnp.maximum(flat - 1, 0)
    nxt = jnp.minimum(flat + 1, last)

    @pl.when(flat > 0)
    def _():
        pl.semaphore_signal(bar, inc=1, device_id=(prev // chs, prev % chs), device_id_type=MESH)

    @pl.when(flat < last)
    def _():
        pl.semaphore_signal(bar, inc=1, device_id=(nxt // chs, nxt % chs), device_id_type=MESH)

    loads[0].wait()
    loads[1].wait()

    cb = 32

    def mask_step(k, carry):
        s = pl.ds(pl.multiple_of(k * cb, cb), cb)
        p = pre_v[s, 0].astype(jnp.float32)
        c = cot_v[s, 0]
        m_nat[s] = jnp.where(p > 0, c.astype(jnp.float32), 0.0).astype(jnp.bfloat16)
        return carry

    lax.fori_loop(0, c_out // cb, mask_step, 0)
    peers = chips + chs - 1 + jnp.minimum(flat, 1) + jnp.minimum(last - flat, 1)
    pl.semaphore_wait(bar, peers)

    halo = pltpu.make_async_remote_copy(
        src_ref=m_nat, dst_ref=h_nat, send_sem=halo_s, recv_sem=halo_r,
        device_id=(prev // chs, prev % chs), device_id_type=MESH,
    )

    @pl.when(flat > 0)
    def _():
        halo.start()

    lane = lax.broadcasted_iota(jnp.int32, (c_out, LANES), 1)

    def relayout_mask(src, dst):
        dst[:, span:] = jnp.zeros((2 * c_out, LANES), jnp.bfloat16)
        m32[:, :rows, :] = src[...].astype(jnp.float32)
        flat32 = m32.reshape(c_out * 16, LANES)
        for b in range(rows):
            v = flat32[pl.ds(b, c_out, stride=16), :]
            dst[:c_out, b * LANES:(b + 1) * LANES] = v.astype(jnp.bfloat16)
            r = jnp.where(lane == LANES - 1, 0.0, pltpu.roll(v, LANES - 1, 1))
            dst[c_out:, b * LANES:(b + 1) * LANES] = r.astype(jnp.bfloat16)

    relayout_mask(m_nat, mh)
    loads[2].wait()

    def feat_step(q, carry):
        p, t, s = q // 4, (q // 2) % 2, q % 2
        buf = f32s.at[q]
        buf[:, :rows, :] = feat_v[:, p, s, t].astype(jnp.float32)
        flat32 = buf.reshape(c_in * 16, LANES)
        for b in range(rows):
            feat_a[q, :, b * LANES:(b + 1) * LANES] = flat32[
                pl.ds(b, c_in, stride=16), :
            ].astype(jnp.bfloat16)
        return carry

    lax.fori_loop(0, 8, feat_step, 0)

    kd_slot = {1: 0, 2: 1, 0: 2}
    ups = c_in // UNIT

    def unit_of(order):
        if order < taps_first:
            return order * ups
        return chunks[1][0] + (order - taps_first) * ups

    def put(kd, kh, kw, val):
        base = unit_of(kd_slot[kd] * 9 + kh * 3 + kw)
        grad[base:base + ups] = val.reshape(ups, UNIT, c_out)

    def wgrad(kd, p, mm):
        dn = (((1,), (1,)), ((), ()))
        t1 = feat_a[p * 4 + 2:p * 4 + 4].reshape(2 * c_in, span)
        o = lax.dot_general(t1, mm[:, :span], dn, preferred_element_type=jnp.float32)
        put(kd, 1, 2, o[:c_in, :c_out])
        put(kd, 1, 0, o[:c_in, c_out:])
        put(kd, 2, 2, o[c_in:, :c_out])
        put(kd, 2, 0, o[c_in:, c_out:])
        t0 = feat_a[p * 4:p * 4 + 2].reshape(2 * c_in, span)
        o = lax.dot_general(t0, mm[:c_out, :span], dn, preferred_element_type=jnp.float32)
        put(kd, 1, 1, o[:c_in])
        put(kd, 2, 1, o[c_in:])
        o = lax.dot_general(feat_a[p * 4 + 3], mm[:, LANES:], dn, preferred_element_type=jnp.float32)
        put(kd, 0, 2, o[:, :c_out])
        put(kd, 0, 0, o[:, c_out:])
        o = lax.dot_general(feat_a[p * 4 + 1], mm[:c_out, LANES:], dn, preferred_element_type=jnp.float32)
        put(kd, 0, 1, o)

    def tap(kd, kh, kw):
        return w_v[kd * 9 + kh * 3 + kw]

    def pair(kd, kh):
        return jnp.concatenate([tap(kd, kh, 2), tap(kd, kh, 0)], 1)

    def dgrad_terms(kd, mm, col):
        def dot(a, b):
            return jnp.dot(a, b, preferred_element_type=jnp.float32)
        here = pl.ds(col, 2 * LANES)
        down = pl.ds(pl.multiple_of(col + LANES, LANES), 2 * LANES)
        t1 = dot(jnp.concatenate([pair(kd, 1), pair(kd, 2)], 0), mm[:, here])
        t1d = dot(pair(kd, 0), mm[:, down])
        t0 = dot(jnp.concatenate([tap(kd, 1, 1), tap(kd, 2, 1)], 0), mm[:c_out, here])
        t0d = dot(tap(kd, 0, 1), mm[:c_out, down])
        return {
            (0, 0): t0[:c_in], (1, 0): t0[c_in:] + t0d,
            (0, 1): t1[:c_in], (1, 1): t1[c_in:] + t1d,
        }

    def dgrad(p, terms):
        def step(k, carry):
            col = pl.multiple_of(k * 2 * LANES, 2 * LANES)
            total = None
            for kd, mm in terms:
                got = dgrad_terms(kd, mm, col)
                total = got if total is None else {key: total[key] + got[key] for key in got}
            for (s, t), val in total.items():
                flat32 = f32s.at[p * 4 + s * 2 + t].reshape(c_in * 16, LANES)
                for j in range(2):
                    flat32[pl.ds(2 * k + j, c_in, stride=16), :] = val[:, j * LANES:(j + 1) * LANES]
            return carry

        lax.fori_loop(0, rows // 2, step, 0)

        def emit(q, carry):
            dg_v[:, p, q // 2, q % 2] = f32s[p * 4 + q, :, :rows, :].astype(jnp.bfloat16)
            return carry

        lax.fori_loop(0, 4, emit, 0)
        return pltpu.make_async_copy(dg_v.at[:, p], dg_hbm.at[:, p], out_sem.at[p])

    class Reduce:
        def __init__(self, idx, base, u):
            self.i, self.base, self.u = idx, base, u
            self.zu = u * chs
            self.half = self.zu * chips
            self.copies = {}

        def remote(self, stage, k, src, dst, dev):
            sem = stage_base[stage] + k
            return pltpu.make_async_remote_copy(
                src_ref=src, dst_ref=dst, send_sem=sA.at[self.i, sem], recv_sem=rA.at[self.i, sem],
                device_id=dev, device_id_type=MESH)

        def chip_dev(self, k):
            return (((chip + k) % chips) * 2 + core, ch)

        def ch_dev(self, k):
            return (sp, (ch + k) % chs)

        def off(self, a, b, c):
            return self.base + (a * self.half) + b * self.zu + c * self.u

        def start(self, stage):
            cps = []
            other = (sp + 1 - 2 * core, ch)
            if stage == 1:
                cps.append(self.remote(1, 0, grad.at[pl.ds(self.off(1 - core, 0, 0), self.half)], r1.at[self.i, pl.ds(0, self.half)], other))
            elif stage == 2:
                for k in range(1, chips):
                    to = (chip + k) % chips
                    cps.append(self.remote(2, k - 1, grad.at[pl.ds(self.off(core, to, 0), self.zu)], r2.at[self.i, k - 1, pl.ds(0, self.zu)], self.chip_dev(k)))
            elif stage == 3:
                for k in range(1, chs):
                    to = (ch + k) % chs
                    cps.append(self.remote(3, k - 1, grad.at[pl.ds(self.off(core, chip, to), self.u)], r3.at[self.i, k - 1, pl.ds(0, self.u)], self.ch_dev(k)))
            elif stage == 4:
                ref = out_v.at[pl.ds(self.off(core, chip, ch), self.u)]
                for k in range(1, chs):
                    cps.append(self.remote(4, k - 1, ref, ref, self.ch_dev(k)))
            elif stage == 5:
                ref = out_v.at[pl.ds(self.off(core, chip, 0), self.zu)]
                for k in range(1, chips):
                    cps.append(self.remote(5, k - 1, ref, ref, self.chip_dev(k)))
            else:
                ref = out_v.at[pl.ds(self.off(core, 0, 0), self.half)]
                cps.append(self.remote(6, 0, ref, ref, other))
            for c in cps:
                c.start()
            self.copies[stage] = cps

        def finish(self, stage):
            for c in self.copies[stage]:
                c.wait_send()
                c.wait_recv()
            if stage == 1:
                s = pl.ds(self.off(core, 0, 0), self.half)
                grad[s] = grad[s] + r1[self.i, :self.half]
            elif stage == 2:
                s = pl.ds(self.off(core, chip, 0), self.zu)
                v = grad[s]
                for k in range(chips - 1):
                    v = v + r2[self.i, k, :self.zu]
                grad[s] = v
            elif stage == 3:
                s = pl.ds(self.off(core, chip, ch), self.u)
                v = grad[s]
                for k in range(chs - 1):
                    v = v + r3[self.i, k, :self.u]
                out_v[s] = v * scale

    stage_base = {1: 0, 2: 1, 3: chips, 4: chips + chs - 1, 5: chips + 2 * chs - 2, 6: 2 * chips + 2 * chs - 3}
    red_a = Reduce(0, *chunks[0])
    red_b = Reduce(1, *chunks[1])

    for lo, hi in ((taps_first * ups, chunks[1][0]), (unit_of(27), grad.shape[0])):
        if lo < hi:
            grad[lo:hi] = jnp.zeros((hi - lo, UNIT, LANES), jnp.float32)

    wgrad(1, 0, mh)
    wgrad(2, 1, mh)
    red_a.start(1)
    loads[3].wait()
    out0 = dgrad(0, [(1, mh)])
    out0.start()
    red_a.finish(1)
    red_a.start(2)

    @pl.when(flat > 0)
    def _():
        halo.wait_send()

    @pl.when(flat < last)
    def _():
        halo.wait_recv()

    @pl.when(flat == last)
    def _():
        h_nat[...] = jnp.zeros_like(h_nat)

    relayout_mask(h_nat, mn)
    wgrad(0, 1, mn)
    red_b.start(1)
    red_a.finish(2)
    red_a.start(3)
    out1 = dgrad(1, [(2, mh), (0, mn)])
    out1.start()
    red_b.finish(1)
    red_b.start(2)
    red_a.finish(3)
    red_a.start(4)
    red_b.finish(2)
    red_b.start(3)
    red_a.finish(4)
    red_a.start(5)
    red_b.finish(3)
    red_b.start(4)
    red_a.finish(5)
    red_a.start(6)
    red_b.finish(4)
    red_b.start(5)
    red_a.finish(6)
    red_b.finish(5)
    red_b.start(6)
    red_b.finish(6)
    outs = []
    for k, (order, count, tap0) in enumerate(
        ((0, taps_first, 9), (taps_first, 18 - taps_first, 9 + taps_first), (18, 9, 0))
    ):
        outs.append(
            pltpu.make_async_copy(
                out_v.at[pl.ds(unit_of(order), count * ups)],
                wg_hbm.at[pl.ds(tap0 * ups, count * ups)],
                out_sem.at[2 + k],
            )
        )
        outs[-1].start()
    out0.wait()
    out1.wait()
    for out in outs:
        out.wait()


def on_device(features, pre_act, cotangent, weight):
    c_in, planes_in, _, _, rows, cols = features.shape
    c_out, planes = pre_act.shape[:2]
    taps = weight.shape[0]
    chips = lax.axis_size("sp") // 2
    chs = lax.axis_size("ch")
    devices = chips * 2 * chs
    scale = 1.0 / math.sqrt(devices * planes * rows * cols)
    ups = c_in // UNIT
    total = taps * ups
    taps_first = 16
    u_a = -(-(taps_first * ups) // devices)
    u_b = -(-(total - taps_first * ups) // devices)
    chunks = ((0, u_a), (u_a * devices, u_b))
    units = (u_a + u_b) * devices
    u_max = max(u_a, u_b)
    n_sems = 2 * chips + 2 * chs - 2
    cfg = (chips, chs, rows, c_in, c_out, scale, chunks, taps_first)
    bf, f32 = jnp.bfloat16, jnp.float32
    span = rows * cols
    any_spec = pl.BlockSpec(memory_space=pl.ANY)
    dg, wg = pl.pallas_call(
        functools.partial(kernel, cfg),
        out_shape=(
            jax.ShapeDtypeStruct(features.shape, bf),
            jax.ShapeDtypeStruct((total, UNIT, c_out), f32),
        ),
        in_specs=[any_spec] * 4,
        out_specs=(any_spec, any_spec),
        scratch_shapes=[
            pltpu.VMEM(pre_act.shape, bf),
            pltpu.VMEM(cotangent.shape, bf),
            pltpu.VMEM(features.shape, bf),
            pltpu.VMEM(weight.shape, bf),
            pltpu.VMEM((c_out, rows, cols), bf),
            pltpu.VMEM((c_out, rows, cols), bf),
            pltpu.VMEM((8, c_in, 16, cols), f32),
            pltpu.VMEM((c_out, 16, cols), f32),
            pltpu.VMEM((2 * c_out, span + cols), bf),
            pltpu.VMEM((2 * c_out, span + cols), bf),
            pltpu.VMEM((8, c_in, span), bf),
            pltpu.VMEM(features.shape, bf),
            pltpu.VMEM((units, UNIT, c_out), f32),
            pltpu.VMEM((units, UNIT, c_out), f32),
            pltpu.VMEM((2, u_max * chs * chips, UNIT, c_out), f32),
            pltpu.VMEM((2, max(1, chips - 1), u_max * chs, UNIT, c_out), f32),
            pltpu.VMEM((2, max(1, chs - 1), u_max, UNIT, c_out), f32),
            pltpu.SemaphoreType.DMA((4,)),
            pltpu.SemaphoreType.DMA((5,)),
            pltpu.SemaphoreType.DMA,
            pltpu.SemaphoreType.DMA,
            pltpu.SemaphoreType.DMA((2, n_sems)),
            pltpu.SemaphoreType.DMA((2, n_sems)),
        ],
        compiler_params=pltpu.CompilerParams(
            collective_id=0, has_side_effects=True, vmem_limit_bytes=56 * 2**20
        ),
    )(pre_act, cotangent, features, weight)
    return dg, wg.reshape(taps, c_in, c_out)


def solution(mesh):
    return jax.shard_map(
        on_device,
        mesh=mesh,
        in_specs=(
            P(None, ("sp", "ch"), None, None, None, None),
            P(None, ("sp", "ch"), None, None),
            P(None, ("sp", "ch"), None, None),
            P(),
        ),
        out_specs=(P(None, ("sp", "ch"), None, None, None, None), P()),
        check_vma=False,
    )
```

time: 185 us -> 52.5 us (0.28)
  waiting for transfers between devices: 68.2 us -> 0 us
  Pallas kernels: 0 us -> 39.6 us
  local copies, waits for them, and re-layouts: 49.3 us -> 12 us
  blocking collectives: 20.9 us -> 0 us
  matrix products: 17.5 us -> 0 us
  between operations: 14.6 us -> 0.66 us
  starting transfers between devices: 8.1 us -> 0 us
  other arithmetic: 4.44 us -> 0 us
    psum x1 -> x0, waiting for transfers between devices: 50.1 us -> none  [on_device(): share = lax.psum(grouped, 'sp')]
    pallas_call x0 -> x1, Pallas kernels: none -> 39.6 us  [on_device(): pl.pallas_call(functools.partial(kernel, cfg), out_shape=(jax.ShapeDtypeS...]
    all_gather x1 -> x0, blocking collectives: 20.9 us -> none  [on_device(): summed = lax.all_gather(share, 'ch', axis=1, tiled=True)]
    reduce_scatter x1 -> x0, waiting for transfers between devices: 18.1 us -> none  [on_device(): grouped = lax.psum_scatter(grad_part, 'ch', scatter_dimension=1, tiled=True)]
    slice x8 -> x0, local copies, waits for them, and re-layouts: 17.9 us -> none  [the longest x2 17.4 us: weight_terms(): tap_rows = plane[:, row_par, col_par].reshape(plane.shape[0], -1)]
    dot_general x35 -> x0, matrix products: 17.5 us -> none  [the longest x8 11.9 us: data_terms(): jnp.dot(w_rows, jnp.concatenate(pair[1], 0), preferred_element_type=jnp.f...]
    ppermute x2 -> x0, starting transfers between devices: 7.8 us -> none  [shifted_2(): return lax.ppermute(block, axis, route)]
    another operation x8 -> x0, local copies, waits for them, and re-layouts: 7.39 us -> none  [data_terms(): jnp.stack([results[depth_par, row_par, 0], results[depth_par, row_par, 1]...]
  transfers between devices with their start and end apart: 4 -> 0, of which waited for: 2 -> 0; matrix products, arithmetic and copies ran while one was open for 28% -> 0% of each run, Pallas kernels for 0% -> 0%
where the time goes in v1:
time: 52.5 us; the launch traced here: 52.3 us
  Pallas kernels  39.6 us (75%)
  local copies, waits for them, and re-layouts  12 us (23%)
  between operations  0.66 us (1%)
    pallas_call x1, Pallas kernels, on_device(): pl.pallas_call(functools.partial(kernel, cfg), out_shape=(jax.ShapeDtypeS...  39.6 us
    unnamed x9, local copies, waits for them, and re-layouts  12 us

profile of v1, /device:TPU:0, one launch (start us, length us, event | category | flops | bytes accessed | tf_op | source)
XLA Modules:
  0.0 52.3 jit_solution(7778658423208574788)
XLA Ops:
  0.6 0.0 copy-start
  0.6 2.3 %copy.6.pre_hbm = bf16[128,1,14,128]{3,2,1,0:T(8,128)(2,1)} copy(bf16[128,1,14,128]{3,0,2,1:T(8,128)(2,1)} %param.5) | data formatting | bytes 917504 | tf_op args[1]
  2.9 2.1 %copy.7.cot_hbm = bf16[128,1,14,128]{3,2,1,0:T(8,128)(2,1)} copy(bf16[128,1,14,128]{3,0,2,1:T(8,128)(2,1)} %param.6) | data formatting | bytes 917504 | tf_op args[2]
  5.0 0.0 copy-done
  5.0 1.9 %copy.8.feat_hbm = bf16[64,2,2,2,14,128]{5,4,3,2,1,0:T(8,128)(2,1)} copy(bf16[64,2,2,2,14,128]{5,3,4,2,1,0:T(2,128)(2,1)S(1)} %copy-done) | data formatting | bytes 3670016 | tf_op args[0]
  6.9 39.6 %shard_map.59 = (bf16[64,2,2,2,14,128]{5,4,3,2,1,0:T(8,128)(2,1)}, f32[216,8,128]{2,1,0:T(8,128)}) custom-call(bf16[128,1,14,128]{3,2,1,0:T(8,128)(2,1)} %copy.6.pre_hbm, bf16[128,1,14,128]{3,2,1,0:T(8,128)(2,1)} %copy.7.cot_hbm, bf16[64,2,2,2,14,128]{5,4,3,2,1,0:T(8,128)(2,1)} %copy.8.feat_hbm, bf16[27,64,128]{2,1,0:T(8,128)(2,1)} %w_hbm.1), custom_call_target="tpu_custom_call" | custom-call | tf_op jit(solution)/shard_map/pallas_call | solution.py:343
  46.6 0.0 copy-start.1
  46.6 4.8 %copy.9 = bf16[64,2,2,2,14,128]{5,3,4,2,1,0:T(2,128)(2,1)} copy(bf16[64,2,2,2,14,128]{5,4,3,2,1,0:T(8,128)(2,1)} %get-tuple-element.6) | data formatting | bytes 3670016
  51.4 0.0 copy-done.1
  51.4 0.9 %copy.11 = f32[27,64,128]{2,1,0:T(8,128)} copy(f32[27,64,128]{2,1,0:T(8,128)S(1)} %bitcast.1) | data formatting | bytes 1769472
Async XLA Ops:
  0.6 4.4 %copy-start = (bf16[64,2,2,2,14,128]{5,3,4,2,1,0:T(2,128)(2,1)S(1)}, bf16[64,2,2,2,14,128]{5,3,4,2,1,0:T(2,128)(2,1)}, u32[]{:S(2)}) copy-start(bf16[64,2,2,2,14,128]{5,3,4,2,1,0:T(2,128)(2,1)} %param.4) | copy-start | bytes 5505028
  46.6 4.8 %copy-start.1 = (f32[216,8,128]{2,1,0:T(8,128)S(1)}, f32[216,8,128]{2,1,0:T(8,128)}, u32[]{:S(2)}) copy-start(f32[216,8,128]{2,1,0:T(8,128)} %get-tuple-element.5) | copy-start | bytes 2654212

commit v2 on v1

--- a/solution.py
+++ b/solution.py
@@ -14,9 +14,9 @@
 
 
 def kernel(cfg, pre_hbm, cot_hbm, feat_hbm, w_hbm, dg_hbm, wg_hbm, *scr):
-    (pre_v, cot_v, feat_v, w_v, m_nat, h_nat, f32s, m32, mh, mn, feat_a, dg_v, grad, out_v) = scr[:14]
-    r1, r2, r3 = scr[14:17]
-    in_sem, out_sem, halo_s, halo_r, sA, rA = scr[17:]
+    (pre_v, cot_v, feat_v, w_v, m_nat, h_nat, mh, mn, feat_a, wl, wf, ws, dg_v, grad, out_v) = scr[:15]
+    r1, r2, r3 = scr[15:18]
+    in_sem, out_sem, halo_s, halo_r, sA, rA = scr[18:]
     chips, chs, rows, c_in, c_out, scale, chunks, taps_first = cfg
     sp = lax.axis_index("sp")
     ch = lax.axis_index("ch")
@@ -27,13 +27,19 @@
     span = rows * LANES
 
     loads = [
-        pltpu.make_async_copy(pre_hbm, pre_v, in_sem.at[0]),
-        pltpu.make_async_copy(cot_hbm, cot_v, in_sem.at[1]),
-        pltpu.make_async_copy(feat_hbm, feat_v, in_sem.at[2]),
-        pltpu.make_async_copy(w_hbm, w_v, in_sem.at[3]),
+        pltpu.make_async_copy(pre_hbm.at[0], pre_v, in_sem.at[0]),
+        pltpu.make_async_copy(cot_hbm.at[0], cot_v, in_sem.at[1]),
+        pltpu.make_async_copy(w_hbm, w_v, in_sem.at[2]),
     ]
     for ld in loads:
         ld.start()
+
+    def load_feat(k, carry):
+        p, s, b = k // (2 * rows), (k // rows) % 2, k % rows
+        pltpu.make_async_copy(feat_hbm.at[:, p, s, b], feat_v.at[p, s, b], in_sem.at[3]).start()
+        return carry
+
+    lax.fori_loop(0, 4 * rows, load_feat, 0)
 
     bar = pltpu.get_barrier_semaphore()
     pl.semaphore_signal(bar, inc=1, device_id=(sp + 1 - 2 * core, ch), device_id_type=MESH)
@@ -55,16 +61,12 @@
     loads[0].wait()
     loads[1].wait()
 
-    cb = 32
-
-    def mask_step(k, carry):
-        s = pl.ds(pl.multiple_of(k * cb, cb), cb)
-        p = pre_v[s, 0].astype(jnp.float32)
-        c = cot_v[s, 0]
-        m_nat[s] = jnp.where(p > 0, c.astype(jnp.float32), 0.0).astype(jnp.bfloat16)
+    def mask_step(b, carry):
+        p = pre_v[b].astype(jnp.float32)
+        m_nat[b] = jnp.where(p > 0, cot_v[b].astype(jnp.float32), 0.0).astype(jnp.bfloat16)
         return carry
 
-    lax.fori_loop(0, c_out // cb, mask_step, 0)
+    lax.fori_loop(0, rows, mask_step, 0)
     peers = chips + chs - 1 + jnp.minimum(flat, 1) + jnp.minimum(last - flat, 1)
     pl.semaphore_wait(bar, peers)
 
@@ -79,31 +81,28 @@
 
     lane = lax.broadcasted_iota(jnp.int32, (c_out, LANES), 1)
 
-    def relayout_mask(src, dst):
+    def spread(src, dst):
         dst[:, span:] = jnp.zeros((2 * c_out, LANES), jnp.bfloat16)
-        m32[:, :rows, :] = src[...].astype(jnp.float32)
-        flat32 = m32.reshape(c_out * 16, LANES)
         for b in range(rows):
-            v = flat32[pl.ds(b, c_out, stride=16), :]
-            dst[:c_out, b * LANES:(b + 1) * LANES] = v.astype(jnp.bfloat16)
-            r = jnp.where(lane == LANES - 1, 0.0, pltpu.roll(v, LANES - 1, 1))
+            v = src[b]
+            dst[:c_out, b * LANES:(b + 1) * LANES] = v
+            r = jnp.where(lane == LANES - 1, 0.0, pltpu.roll(v.astype(jnp.float32), LANES - 1, 1))
             dst[c_out:, b * LANES:(b + 1) * LANES] = r.astype(jnp.bfloat16)
 
-    relayout_mask(m_nat, mh)
-    loads[2].wait()
-
-    def feat_step(q, carry):
-        p, t, s = q // 4, (q // 2) % 2, q % 2
-        buf = f32s.at[q]
-        buf[:, :rows, :] = feat_v[:, p, s, t].astype(jnp.float32)
-        flat32 = buf.reshape(c_in * 16, LANES)
+    spread(m_nat, mh)
+    pltpu.make_async_copy(feat_v, feat_v, in_sem.at[3]).wait()
+    two = 2 * c_in
+
+    feat_rows = feat_v.reshape(2, 2, rows, two, LANES)
+
+    def feat_step(k, carry):
+        p, s = k // 2, k % 2
+        at = pl.ds(pl.multiple_of(s * two, two), two)
         for b in range(rows):
-            feat_a[q, :, b * LANES:(b + 1) * LANES] = flat32[
-                pl.ds(b, c_in, stride=16), :
-            ].astype(jnp.bfloat16)
+            feat_a[p, at, b * LANES:(b + 1) * LANES] = feat_rows[p, s, b]
         return carry
 
-    lax.fori_loop(0, 8, feat_step, 0)
+    lax.fori_loop(0, 4, feat_step, 0)
 
     kd_slot = {1: 0, 2: 1, 0: 2}
     ups = c_in // UNIT
@@ -119,63 +118,50 @@
 
     def wgrad(kd, p, mm):
         dn = (((1,), (1,)), ((), ()))
-        t1 = feat_a[p * 4 + 2:p * 4 + 4].reshape(2 * c_in, span)
-        o = lax.dot_general(t1, mm[:, :span], dn, preferred_element_type=jnp.float32)
-        put(kd, 1, 2, o[:c_in, :c_out])
-        put(kd, 1, 0, o[:c_in, c_out:])
-        put(kd, 2, 2, o[c_in:, :c_out])
-        put(kd, 2, 0, o[c_in:, c_out:])
-        t0 = feat_a[p * 4:p * 4 + 2].reshape(2 * c_in, span)
-        o = lax.dot_general(t0, mm[:c_out, :span], dn, preferred_element_type=jnp.float32)
-        put(kd, 1, 1, o[:c_in])
-        put(kd, 2, 1, o[c_in:])
-        o = lax.dot_general(feat_a[p * 4 + 3], mm[:, LANES:], dn, preferred_element_type=jnp.float32)
-        put(kd, 0, 2, o[:, :c_out])
-        put(kd, 0, 0, o[:, c_out:])
-        o = lax.dot_general(feat_a[p * 4 + 1], mm[:c_out, LANES:], dn, preferred_element_type=jnp.float32)
-        put(kd, 0, 1, o)
-
-    def tap(kd, kh, kw):
-        return w_v[kd * 9 + kh * 3 + kw]
-
-    def pair(kd, kh):
-        return jnp.concatenate([tap(kd, kh, 2), tap(kd, kh, 0)], 1)
-
-    def dgrad_terms(kd, mm, col):
-        def dot(a, b):
-            return jnp.dot(a, b, preferred_element_type=jnp.float32)
-        here = pl.ds(col, 2 * LANES)
-        down = pl.ds(pl.multiple_of(col + LANES, LANES), 2 * LANES)
-        t1 = dot(jnp.concatenate([pair(kd, 1), pair(kd, 2)], 0), mm[:, here])
-        t1d = dot(pair(kd, 0), mm[:, down])
-        t0 = dot(jnp.concatenate([tap(kd, 1, 1), tap(kd, 2, 1)], 0), mm[:c_out, here])
-        t0d = dot(tap(kd, 0, 1), mm[:c_out, down])
-        return {
-            (0, 0): t0[:c_in], (1, 0): t0[c_in:] + t0d,
-            (0, 1): t1[:c_in], (1, 1): t1[c_in:] + t1d,
-        }
+        o = lax.dot_general(feat_a[p], mm[:, :span], dn, preferred_element_type=jnp.float32)
+        d = lax.dot_general(feat_a[p, two:], mm[:, LANES:], dn, preferred_element_type=jnp.float32)
+        for r in range(2):
+            ws[r, :2 * two] = o[:, r * c_out:(r + 1) * c_out]
+            ws[r, 2 * two:] = d[:, r * c_out:(r + 1) * c_out]
+        for kh, part in ((1, 0), (2, 1), (0, 2)):
+            for kw, r, t in ((1, 0, 0), (2, 0, 1), (0, 1, 1)):
+                put(kd, kh, kw, ws[r, pl.ds(part * two + t, c_in, stride=2), :])
+
+    def weights():
+        def step(kd, carry):
+            for part, kh in enumerate((1, 2, 0)):
+                base = kd * 9 + kh * 3
+                wf[0, pl.ds(0, c_in, stride=2), :] = w_v[base + 1].astype(jnp.float32)
+                wf[0, pl.ds(1, c_in, stride=2), :] = w_v[base + 2].astype(jnp.float32)
+                wf[1, pl.ds(0, c_in, stride=2), :] = jnp.zeros((c_in, c_out), jnp.float32)
+                wf[1, pl.ds(1, c_in, stride=2), :] = w_v[base].astype(jnp.float32)
+                for r in range(2):
+                    wl[kd, part * two:(part + 1) * two, r * c_out:(r + 1) * c_out] = wf[r].astype(jnp.bfloat16)
+            return carry
+
+        lax.fori_loop(0, 3, step, 0)
+
+    dg_rows = dg_v.reshape(2, 2, rows, two, LANES)
 
     def dgrad(p, terms):
         def step(k, carry):
             col = pl.multiple_of(k * 2 * LANES, 2 * LANES)
-            total = None
+            here = pl.ds(col, 2 * LANES)
+            down = pl.ds(pl.multiple_of(col + LANES, LANES), 2 * LANES)
+            top, bot = None, None
             for kd, mm in terms:
-                got = dgrad_terms(kd, mm, col)
-                total = got if total is None else {key: total[key] + got[key] for key in got}
-            for (s, t), val in total.items():
-                flat32 = f32s.at[p * 4 + s * 2 + t].reshape(c_in * 16, LANES)
+                o = jnp.dot(wl[kd, :2 * two], mm[:, here], preferred_element_type=jnp.float32)
+                d = jnp.dot(wl[kd, 2 * two:], mm[:, down], preferred_element_type=jnp.float32)
+                top = o[:two] if top is None else top + o[:two]
+                bot = o[two:] + d if bot is None else bot + (o[two:] + d)
+            for s, val in ((0, top), (1, bot)):
                 for j in range(2):
-                    flat32[pl.ds(2 * k + j, c_in, stride=16), :] = val[:, j * LANES:(j + 1) * LANES]
+                    b = 2 * k + j
+                    dg_rows[p, s, b] = val[:, j * LANES:(j + 1) * LANES].astype(jnp.bfloat16)
+                    pltpu.make_async_copy(dg_v.at[p, s, b], dg_hbm.at[:, p, s, b], out_sem.at[p]).start()
             return carry
 
         lax.fori_loop(0, rows // 2, step, 0)
-
-        def emit(q, carry):
-            dg_v[:, p, q // 2, q % 2] = f32s[p * 4 + q, :, :rows, :].astype(jnp.bfloat16)
-            return carry
-
-        lax.fori_loop(0, 4, emit, 0)
-        return pltpu.make_async_copy(dg_v.at[:, p], dg_hbm.at[:, p], out_sem.at[p])
 
     class Reduce:
         def __init__(self, idx, base, u):
@@ -258,9 +244,9 @@
     wgrad(1, 0, mh)
     wgrad(2, 1, mh)
     red_a.start(1)
-    loads[3].wait()
-    out0 = dgrad(0, [(1, mh)])
-    out0.start()
+    loads[2].wait()
+    weights()
+    dgrad(0, [(1, mh)])
     red_a.finish(1)
     red_a.start(2)
 
@@ -276,13 +262,12 @@
     def _():
         h_nat[...] = jnp.zeros_like(h_nat)
 
-    relayout_mask(h_nat, mn)
+    spread(h_nat, mn)
     wgrad(0, 1, mn)
     red_b.start(1)
     red_a.finish(2)
     red_a.start(3)
-    out1 = dgrad(1, [(2, mh), (0, mn)])
-    out1.start()
+    dgrad(1, [(2, mh), (0, mn)])
     red_b.finish(1)
     red_b.start(2)
     red_a.finish(3)
@@ -313,8 +298,8 @@
             )
         )
         outs[-1].start()
-    out0.wait()
-    out1.wait()
+    for p in range(2):
+        pltpu.make_async_copy(dg_v.at[p], dg_v.at[p], out_sem.at[p]).wait()
     for out in outs:
         out.wait()
 
@@ -343,24 +328,25 @@
     dg, wg = pl.pallas_call(
         functools.partial(kernel, cfg),
         out_shape=(
-            jax.ShapeDtypeStruct(features.shape, bf),
+            jax.ShapeDtypeStruct((c_in, planes_in, 2, rows, 2, cols), bf),
             jax.ShapeDtypeStruct((total, UNIT, c_out), f32),
         ),
         in_specs=[any_spec] * 4,
         out_specs=(any_spec, any_spec),
         scratch_shapes=[
-            pltpu.VMEM(pre_act.shape, bf),
-            pltpu.VMEM(cotangent.shape, bf),
-            pltpu.VMEM(features.shape, bf),
+            pltpu.VMEM((rows, c_out, cols), bf),
+            pltpu.VMEM((rows, c_out, cols), bf),
+            pltpu.VMEM((2, 2, rows, c_in, 2, cols), bf),
             pltpu.VMEM(weight.shape, bf),
-            pltpu.VMEM((c_out, rows, cols), bf),
-            pltpu.VMEM((c_out, rows, cols), bf),
-            pltpu.VMEM((8, c_in, 16, cols), f32),
-            pltpu.VMEM((c_out, 16, cols), f32),
+            pltpu.VMEM((rows, c_out, cols), bf),
+            pltpu.VMEM((rows, c_out, cols), bf),
             pltpu.VMEM((2 * c_out, span + cols), bf),
             pltpu.VMEM((2 * c_out, span + cols), bf),
-            pltpu.VMEM((8, c_in, span), bf),
-            pltpu.VMEM(features.shape, bf),
+            pltpu.VMEM((2, 4 * c_in, span), bf),
+            pltpu.VMEM((3, 6 * c_in, 2 * c_out), bf),
+            pltpu.VMEM((2, 2 * c_in, c_out), f32),
+            pltpu.VMEM((2, 6 * c_in, c_out), f32),
+            pltpu.VMEM((2, 2, rows, c_in, 2, cols), bf),
             pltpu.VMEM((units, UNIT, c_out), f32),
             pltpu.VMEM((units, UNIT, c_out), f32),
             pltpu.VMEM((2, u_max * chs * chips, UNIT, c_out), f32),
@@ -376,8 +362,13 @@
         compiler_params=pltpu.CompilerParams(
             collective_id=0, has_side_effects=True, vmem_limit_bytes=56 * 2**20
         ),
-    )(pre_act, cotangent, features, weight)
-    return dg, wg.reshape(taps, c_in, c_out)
+    )(
+        pre_act.transpose(1, 2, 0, 3),
+        cotangent.transpose(1, 2, 0, 3),
+        features.transpose(0, 1, 2, 4, 3, 5),
+        weight,
+    )
+    return dg.transpose(0, 1, 2, 4, 3, 5), wg.reshape(taps, c_in, c_out)
 
 
 def solution(mesh):

time: 52.5 us -> 44.8 us (0.85)
  local copies, waits for them, and re-layouts: 12 us -> 4.98 us
  Pallas kernels: 39.6 us -> 39 us
    unnamed x9 -> x4, local copies, waits for them, and re-layouts: 12 us -> 4.98 us
    pallas_call x1, Pallas kernels: 39.6 us -> 39 us  [on_device(): pl.pallas_call(functools.partial(kernel, cfg), out_shape=(jax.ShapeDtypeS...]
where the time goes in v2:
time: 44.8 us; the launch traced here: 44.7 us
  Pallas kernels  39 us (87%)
  local copies, waits for them, and re-layouts  4.98 us (11%)
  between operations  0.65 us (1%)
    pallas_call x1, Pallas kernels, on_device(): pl.pallas_call(functools.partial(kernel, cfg), out_shape=(jax.ShapeDtypeS...  39 us
    unnamed x4, local copies, waits for them, and re-layouts  4.98 us

profile of v2, /device:TPU:0, one launch (start us, length us, event | category | flops | bytes accessed | tf_op | source)
XLA Modules:
  0.0 44.7 jit_solution(13621220789326766807)
XLA Ops:
  0.6 39.0 %shard_map.59 = (bf16[64,2,2,14,2,128]{5,4,3,2,1,0:T(2,128)(2,1)}, f32[216,8,128]{2,1,0:T(8,128)}) custom-call(bf16[1,14,128,128]{3,2,1,0:T(8,128)(2,1)} %bitcast.8, bf16[1,14,128,128]{3,2,1,0:T(8,128)(2,1)} %bitcast.9, bf16[64,2,2,14,2,128]{5,4,3,2,1,0:T(2,128)(2,1)} %bitcast.5, bf16[27,64,128]{2,1,0:T(8,128)(2,1)} %w_hbm.1), custom_call_target="tpu_custom_call" | custom-call | tf_op jit(solution)/shard_map/pallas_call | solution.py:328
  39.7 0.0 copy-start
  39.7 4.1 %copy.8 = bf16[64,2,2,2,14,128]{5,3,4,2,1,0:T(2,128)(2,1)} copy(bf16[64,2,2,2,14,128]{5,3,4,2,1,0:T(2,128)(2,1)} %bitcast.6) | data formatting | bytes 3670016
  43.8 0.0 copy-done
  43.8 0.9 %copy.9 = f32[27,64,128]{2,1,0:T(8,128)} copy(f32[27,64,128]{2,1,0:T(8,128)S(1)} %bitcast.7) | data formatting | bytes 1769472
Async XLA Ops:
  39.7 4.1 %copy-start = (f32[216,8,128]{2,1,0:T(8,128)S(1)}, f32[216,8,128]{2,1,0:T(8,128)}, u32[]{:S(2)}) copy-start(f32[216,8,128]{2,1,0:T(8,128)} %get-tuple-element.5) | copy-start | bytes 2654212

commit v3 on v2

--- a/solution.py
+++ b/solution.py
@@ -158,7 +158,7 @@
                 for j in range(2):
                     b = 2 * k + j
                     dg_rows[p, s, b] = val[:, j * LANES:(j + 1) * LANES].astype(jnp.bfloat16)
-                    pltpu.make_async_copy(dg_v.at[p, s, b], dg_hbm.at[:, p, s, b], out_sem.at[p]).start()
+                    pltpu.make_async_copy(dg_v.at[p, s, b], dg_hbm.at[p, s, b], out_sem.at[p]).start()
             return carry
 
         lax.fori_loop(0, rows // 2, step, 0)
@@ -246,9 +246,11 @@
     red_a.start(1)
     loads[2].wait()
     weights()
-    dgrad(0, [(1, mh)])
     red_a.finish(1)
     red_a.start(2)
+    dgrad(0, [(1, mh)])
+    red_a.finish(2)
+    red_a.start(3)
 
     @pl.when(flat > 0)
     def _():
@@ -263,26 +265,24 @@
         h_nat[...] = jnp.zeros_like(h_nat)
 
     spread(h_nat, mn)
+    red_a.finish(3)
+    red_a.start(4)
     wgrad(0, 1, mn)
     red_b.start(1)
-    red_a.finish(2)
-    red_a.start(3)
-    dgrad(1, [(2, mh), (0, mn)])
+    red_a.finish(4)
+    red_a.start(5)
     red_b.finish(1)
     red_b.start(2)
-    red_a.finish(3)
-    red_a.start(4)
+    dgrad(1, [(2, mh), (0, mn)])
     red_b.finish(2)
     red_b.start(3)
-    red_a.finish(4)
-    red_a.start(5)
+    red_a.finish(5)
+    red_a.start(6)
     red_b.finish(3)
     red_b.start(4)
-    red_a.finish(5)
-    red_a.start(6)
+    red_a.finish(6)
     red_b.finish(4)
     red_b.start(5)
-    red_a.finish(6)
     red_b.finish(5)
     red_b.start(6)
     red_b.finish(6)
@@ -304,6 +304,21 @@
         out.wait()
 
 
+def store_kernel(dg_in, wg_in, dg_out, wg_out, sem):
+    rows = dg_in.shape[2]
+    wg_copy = pltpu.make_async_copy(wg_in, wg_out, sem.at[0])
+    wg_copy.start()
+
+    def step(k, carry):
+        p, s, b = k // (2 * rows), (k // rows) % 2, k % rows
+        pltpu.make_async_copy(dg_in.at[p, s, b], dg_out.at[:, p, s, b], sem.at[1]).start()
+        return carry
+
+    lax.fori_loop(0, 4 * rows, step, 0)
+    pltpu.make_async_copy(dg_in, dg_in, sem.at[1]).wait()
+    wg_copy.wait()
+
+
 def on_device(features, pre_act, cotangent, weight):
     c_in, planes_in, _, _, rows, cols = features.shape
     c_out, planes = pre_act.shape[:2]
@@ -323,15 +338,17 @@
     n_sems = 2 * chips + 2 * chs - 2
     cfg = (chips, chs, rows, c_in, c_out, scale, chunks, taps_first)
     bf, f32 = jnp.bfloat16, jnp.float32
+    held = 2 * (units + u_max * chs * chips + chips * u_max * chs + chs * u_max)
+    vmem = 17 * 2**20 + held * UNIT * c_out * 4
     span = rows * cols
     any_spec = pl.BlockSpec(memory_space=pl.ANY)
     dg, wg = pl.pallas_call(
         functools.partial(kernel, cfg),
         out_shape=(
-            jax.ShapeDtypeStruct((c_in, planes_in, 2, rows, 2, cols), bf),
+            jax.ShapeDtypeStruct((2, 2, rows, c_in, 2, cols), bf),
             jax.ShapeDtypeStruct((total, UNIT, c_out), f32),
         ),
-        in_specs=[any_spec] * 4,
+        in_specs=[pl.BlockSpec(memory_space=pltpu.HBM)] * 4,
         out_specs=(any_spec, any_spec),
         scratch_shapes=[
             pltpu.VMEM((rows, c_out, cols), bf),
@@ -360,14 +377,25 @@
             pltpu.SemaphoreType.DMA((2, n_sems)),
         ],
         compiler_params=pltpu.CompilerParams(
-            collective_id=0, has_side_effects=True, vmem_limit_bytes=56 * 2**20
+            collective_id=0, has_side_effects=True, vmem_limit_bytes=vmem
         ),
     )(
-        pre_act.transpose(1, 2, 0, 3),
-        cotangent.transpose(1, 2, 0, 3),
-        features.transpose(0, 1, 2, 4, 3, 5),
-        weight,
+        pltpu.with_memory_space_constraint(pre_act.transpose(1, 2, 0, 3), pltpu.HBM),
+        pltpu.with_memory_space_constraint(cotangent.transpose(1, 2, 0, 3), pltpu.HBM),
+        pltpu.with_memory_space_constraint(features.transpose(0, 1, 2, 4, 3, 5), pltpu.HBM),
+        pltpu.with_memory_space_constraint(weight, pltpu.HBM),
     )
+    dg, wg = pl.pallas_call(
+        store_kernel,
+        out_shape=(
+            jax.ShapeDtypeStruct((c_in, planes_in, 2, rows, 2, cols), bf),
+            jax.ShapeDtypeStruct(wg.shape, f32),
+        ),
+        in_specs=[any_spec] * 2,
+        out_specs=(pl.BlockSpec(memory_space=pltpu.HBM),) * 2,
+        scratch_shapes=[pltpu.SemaphoreType.DMA((2,))],
+        compiler_params=pltpu.CompilerParams(vmem_limit_bytes=2**20),
+    )(dg, wg)
     return dg.transpose(0, 1, 2, 4, 3, 5), wg.reshape(taps, c_in, c_out)
 
 

time: 44.8 us -> 46.9 us (1.047)
  Pallas kernels: 39 us -> 46.2 us
  local copies, waits for them, and re-layouts: 4.98 us -> 0 us
    pallas_call x1, Pallas kernels: 39 us -> 44.4 us  [on_device(): pl.pallas_call(functools.partial(kernel, cfg), out_shape=(jax.ShapeDtypeS...]
    unnamed x4 -> x0, local copies, waits for them, and re-layouts: 4.98 us -> none
    pallas_call x0 -> x1, Pallas kernels: none -> 1.78 us  [on_device(): pl.pallas_call(store_kernel, out_shape=(jax.ShapeDtypeStruct((c_in, plane...]
where the time goes in v3:
time: 46.9 us; the launch traced here: 46.8 us
  Pallas kernels  46.2 us (99%)
  between operations  0.64 us (1%)
    pallas_call x1, Pallas kernels, on_device(): pl.pallas_call(functools.partial(kernel, cfg), out_shape=(jax.ShapeDtypeS...  44.4 us
    pallas_call x1, Pallas kernels, on_device(): pl.pallas_call(store_kernel, out_shape=(jax.ShapeDtypeStruct((c_in, plane...  1.78 us

profile of v3, /device:TPU:0, one launch (start us, length us, event | category | flops | bytes accessed | tf_op | source)
XLA Modules:
  0.0 46.8 jit_solution(5336868966430779541)
XLA Ops:
  0.6 44.4 %shard_map.59 = (bf16[2,2,14,64,2,128]{5,4,3,2,1,0:T(2,128)(2,1)S(1)}, f32[216,8,128]{2,1,0:T(8,128)S(1)}) custom-call(bf16[1,14,128,128]{3,2,1,0:T(8,128)(2,1)} %bitcast.6, bf16[1,14,128,128]{3,2,1,0:T(8,128)(2,1)} %bitcast.7, bf16[64,2,2,14,2,128]{5,4,3,2,1,0:T(2,128)(2,1)} %bitcast.5, bf16[27,64,128]{2,1,0:T(8,128)(2,1)} %w_hbm.1), custom_call_target="tpu_custom_call" | custom-call | tf_op jit(solution)/shard_map/pallas_call | solution.py:345
  45.0 1.8 %shard_map.60 = (bf16[64,2,2,14,2,128]{5,4,3,2,1,0:T(2,128)(2,1)}, f32[216,8,128]{2,1,0:T(8,128)}) custom-call(bf16[2,2,14,64,2,128]{5,4,3,2,1,0:T(2,128)(2,1)S(1)} %get-tuple-element.6.dg_in, f32[216,8,128]{2,1,0:T(8,128)S(1)} %get-tuple-element.7.wg_in), custom_call_target="tpu_custom_call" | custom-call | tf_op jit(solution)/shard_map/pallas_call | solution.py:388

commit v4 on v3

--- a/solution.py
+++ b/solution.py
@@ -246,43 +246,43 @@
     red_a.start(1)
     loads[2].wait()
     weights()
+    dgrad(0, [(1, mh)])
     red_a.finish(1)
     red_a.start(2)
-    dgrad(0, [(1, mh)])
+
+    @pl.when(flat > 0)
+    def _():
+        halo.wait_send()
+
+    @pl.when(flat < last)
+    def _():
+        halo.wait_recv()
+
+    @pl.when(flat == last)
+    def _():
+        h_nat[...] = jnp.zeros_like(h_nat)
+
+    spread(h_nat, mn)
+    wgrad(0, 1, mn)
+    red_b.start(1)
     red_a.finish(2)
     red_a.start(3)
-
-    @pl.when(flat > 0)
-    def _():
-        halo.wait_send()
-
-    @pl.when(flat < last)
-    def _():
-        halo.wait_recv()
-
-    @pl.when(flat == last)
-    def _():
-        h_nat[...] = jnp.zeros_like(h_nat)
-
-    spread(h_nat, mn)
+    dgrad(1, [(2, mh), (0, mn)])
+    red_b.finish(1)
+    red_b.start(2)
     red_a.finish(3)
     red_a.start(4)
-    wgrad(0, 1, mn)
-    red_b.start(1)
+    red_b.finish(2)
+    red_b.start(3)
     red_a.finish(4)
     red_a.start(5)
-    red_b.finish(1)
-    red_b.start(2)
-    dgrad(1, [(2, mh), (0, mn)])
-    red_b.finish(2)
-    red_b.start(3)
+    red_b.finish(3)
+    red_b.start(4)
     red_a.finish(5)
     red_a.start(6)
-    red_b.finish(3)
-    red_b.start(4)
-    red_a.finish(6)
     red_b.finish(4)
     red_b.start(5)
+    red_a.finish(6)
     red_b.finish(5)
     red_b.start(6)
     red_b.finish(6)

time: 46.9 us -> 42.9 us (0.915)
  Pallas kernels: 46.2 us -> 42.1 us
    pallas_call x1, Pallas kernels: 44.4 us -> 40.3 us  [on_device(): pl.pallas_call(functools.partial(kernel, cfg), out_shape=(jax.ShapeDtypeS...]
where the time goes in v4:
time: 42.9 us; the launch traced here: 42.8 us
  Pallas kernels  42.1 us (98%)
  between operations  0.64 us (1%)
    pallas_call x1, Pallas kernels, on_device(): pl.pallas_call(functools.partial(kernel, cfg), out_shape=(jax.ShapeDtypeS...  40.3 us
    pallas_call x1, Pallas kernels, on_device(): pl.pallas_call(store_kernel, out_shape=(jax.ShapeDtypeStruct((c_in, plane...  1.78 us

profile of v4, /device:TPU:0, one launch (start us, length us, event | category | flops | bytes accessed | tf_op | source)
XLA Modules:
  0.0 42.8 jit_solution(2023254744530833720)
XLA Ops:
  0.6 40.3 %shard_map.59 = (bf16[2,2,14,64,2,128]{5,4,3,2,1,0:T(2,128)(2,1)S(1)}, f32[216,8,128]{2,1,0:T(8,128)S(1)}) custom-call(bf16[1,14,128,128]{3,2,1,0:T(8,128)(2,1)} %bitcast.6, bf16[1,14,128,128]{3,2,1,0:T(8,128)(2,1)} %bitcast.7, bf16[64,2,2,14,2,128]{5,4,3,2,1,0:T(2,128)(2,1)} %bitcast.5, bf16[27,64,128]{2,1,0:T(8,128)(2,1)} %w_hbm.1), custom_call_target="tpu_custom_call" | custom-call | tf_op jit(solution)/shard_map/pallas_call | solution.py:345
  41.0 1.8 %shard_map.60 = (bf16[64,2,2,14,2,128]{5,4,3,2,1,0:T(2,128)(2,1)}, f32[216,8,128]{2,1,0:T(8,128)}) custom-call(bf16[2,2,14,64,2,128]{5,4,3,2,1,0:T(2,128)(2,1)S(1)} %get-tuple-element.6.dg_in, f32[216,8,128]{2,1,0:T(8,128)S(1)} %get-tuple-element.7.wg_in), custom_call_target="tpu_custom_call" | custom-call | tf_op jit(solution)/shard_map/pallas_call | solution.py:388
